TPU v7x, 128 devices: a whole 4x4x4 slice. The times are simulated.
128 devices in a mesh: row: 8 (over z, core), col: 16 (over y, x).
Axes of the slice: x: 4, y: 4, z: 4, core: 2. Of those that a mesh axis runs over, the one named last changes fastest.
Arguments:
- left_amps: bfloat16 [8192, 8192], P('row', 'col'), may hold values from -6 to 6
- right_ints: bfloat16 [8192, 16384], P('row', 'col'), may hold values from -0.0625 to 0.0625
- left_mask: int32 [64, 64], P('row', 'col'), may hold values from 0 to 1, as said below
- right_mask: int32 [64, 128], P('row', 'col'), may hold values from 0 to 1, as said below
- result_mask: int32 [64, 128], P('row', 'col'), may hold values from 0 to 1, as said below
Outputs:
- pair_major: bfloat16 [128, 1048576], P(None, ('row', 'col'))
Inputs may be any that keep to these rules, and one draw needn't show every extreme that they name: `left_mask`: a tile is kept (1) or left out (0). `right_mask`: a tile is kept (1) or left out (0). `result_mask`: a tile is kept (1) or left out (0).
All inputs are finite; a program needn't handle non-finite values.
Results may differ from a plain program's by a relative error of at most 0.001.
Values may be sent and summed in bfloat16 or wider, within the bound.
A program may use at most 128 MiB of HBM per device.

v0:
```python
import jax
import jax.numpy as jnp
from jax import lax
from jax.sharding import PartitionSpec as P

TILE = 128


def expand(values, mask):
    rows, cols = values.shape
    tiled = values.reshape(rows // TILE, TILE, cols // TILE, TILE)
    kept = tiled * mask.astype(values.dtype)[:, None, :, None]
    return kept.reshape(rows, cols)


def local(left_amps, right_ints, left_mask, right_mask, result_mask):
    masked_left = expand(left_amps, left_mask)
    masked_right = expand(right_ints, right_mask)
    rows_here = masked_left.shape[0]
    cols_here = masked_right.shape[1]
    whole_left = lax.all_gather(masked_left, "col", axis=1, tiled=True)
    product = jnp.dot(
        whole_left,
        lax.all_gather(masked_right, "row", axis=0, tiled=True),
        preferred_element_type=jnp.float32,
    )
    kept = expand(product, result_mask).astype(jnp.bfloat16)
    n_row = lax.axis_size("row")
    n_col = lax.axis_size("col")
    owners = n_row * n_col
    share = rows_here * cols_here // owners
    pieces = kept.reshape(owners, share)
    return lax.all_to_all(pieces, ("row", "col"), split_axis=0, concat_axis=0, tiled=True)


def solution(mesh):
    in_specs = (P("row", "col"), P("row", "col"), P("row", "col"), P("row", "col"), P("row", "col"))
    out_specs = P(None, ("row", "col"))
    return jax.shard_map(local, mesh=mesh, in_specs=in_specs, out_specs=out_specs, check_vma=False)
```

profile of v0, /device:TPU:1, one launch (start us, length us, event | category | flops | bytes accessed | tf_op | source)
XLA Modules:
  0.0 325.5 jit_solution(3875941070786762936)
XLA Ops:
  6.5 0.7 convert_element_type.13
  7.2 0.3 mul.36
  7.6 0.0 copy-start.2
  7.6 0.0 copy-start
  7.6 3.3 %bitcast_multiply_fusion.1 = bf16[1024,1024]{1,0:T(8,128)(2,1)} fusion(bf16[1024,1024]{1,0:T(8,128)(2,1)} %param.6, bf16[128,8,8,128]{3,2,1,0:T(8,128)(2,1)S(1)} %bitcast.19), kind=kLoop, calls=%fused_computation.2 | loop fusion | flops 1048576 | bytes 6291456 | tf_op jit(solution)/shard_map/mul | solution.py:12
  10.9 0.0 all-gather.5.cloned.1.call-update
  10.9 0.0 all-gather.3.cloned.1.call-start
  10.9 0.0 copy-done.2
  11.0 0.1 copy.9
  11.1 0.3 mul.33
  11.4 0.0 copy-done
  11.4 1.2 bitcast_multiply_fusion.2
  12.6 0.0 all-gather.3.cloned.1.call-update
  12.6 87.2 %all-gather.5.cloned.1.call-done = bf16[8192,1024]{1,0:T(8,128)(2,1)} async-done(((bf16[1024,1024]{1,0:T(8,128)(2,1)}), bf16[8192,1024]{1,0:T(8,128)(2,1)}) %all-gather.5.cloned.1.call-update) | async-done | bytes 16777232 | tf_op jit(solution)/shard_map/all_gather | solution.py:24
  99.9 122.2 %all-gather.3.cloned.1.call-done = bf16[1024,8192]{1,0:T(8,128)(2,1)} async-done(((bf16[1024,512]{1,0:T(8,128)(2,1)}), bf16[1024,8192]{1,0:T(8,128)(2,1)}) %all-gather.3.cloned.1.call-update) | async-done | bytes 16777232 | tf_op jit(solution)/shard_map/all_gather | solution.py:21
  222.1 0.3 mul.39
  222.4 22.4 %fusion = bf16[1024,1024]{1,0:T(8,128)(2,1)S(1)} fusion(f32[128,8,8,128]{3,2,1,0:T(8,128)S(1)} %bitcast.21, bf16[1024,8192]{1,0:T(8,128)(2,1)} %all-gather.3.cloned.1.call-done, bf16[8192,1024]{1,0:T(8,128)(2,1)} %all-gather.5.cloned.1.call-done), kind=kOutput, calls=%fused_computation.1 | convolution fusion | flops 17181966336 | bytes 39845888 | tf_op jit(solution)/shard_map/dot_general | solution.py:22
  244.8 6.5 %all_to_all.11 = bf16[128,1,8192]{2,1,0:T(2,128)(2,1)} reshape(bf16[1024,1024]{1,0:T(8,128)(2,1)S(1)} %fusion) | data formatting | bytes 4194304 | tf_op jit(solution)/shard_map/all_to_all | solution.py:33
  251.3 0.5 broadcast.6
  251.8 13.2 %reduce = bf16[128,8192]{1,0:T(8,128)(2,1)S(1)} reduce(bf16[128,1,8192]{2,1,0:T(2,128)(2,1)} %all_to_all.11, bf16[]{:T(256)} %broadcast.6), dimensions={1}, to_apply=%all_to_all.11.reduce_sub_computation | reduce | bytes 4194306 | tf_op jit(solution)/shard_map/all_to_all | solution.py:33
  265.1 2.8 reshape.16
  267.8 38.3 %all_to_all.13 = bf16[128,2,4096]{2,1,0:T(2,128)(2,1)S(1)} all-to-all(bf16[128,2,4096]{2,1,0:T(2,128)(2,1)} %reshape.16), channel_id=1, replica_groups=mesh['row'=8,'col'=16] {'row','col'}, dimensions={0} | all-to-all | bytes 4194304 | tf_op jit(solution)/shard_map/all_to_all | solution.py:33
  306.1 6.7 %reshape.17 = bf16[128,1,8192]{2,1,0:T(2,128)(2,1)} reshape(bf16[128,2,4096]{2,1,0:T(2,128)(2,1)S(1)} %all_to_all.13) | data formatting | bytes 4194304
  312.8 5.8 %copy.19 = bf16[128,1,8192]{2,0,1:T(8,128)(2,1)} copy(bf16[128,1,8192]{2,1,0:T(2,128)(2,1)} %reshape.17) | data formatting | bytes 4194304
  (5 shorter events, 0.0 us)
Async XLA Ops:
  6.5 93.3 %all-gather.5.cloned.1.call-start = ((), (), s32[]{:S(2)}) async-start(), calls=%async_computation.2 | async-start | bytes 18874368 | tf_op jit(solution)/shard_map/all_gather | solution.py:24
  7.6 3.4 %copy-start.2 = (s32[8,4]{0,1:T(4,128)S(1)}, s32[8,4]{0,1:T(4,128)}, u32[]{:S(2)}) copy-start(s32[8,4]{0,1:T(4,128)} %param.7) | copy-start | bytes 388
  7.6 3.8 %copy-start = (bf16[1024,512]{1,0:T(8,128)(2,1)S(1)}, bf16[1024,512]{1,0:T(8,128)(2,1)}, u32[]{:S(2)}) copy-start(bf16[1024,512]{1,0:T(8,128)(2,1)} %param.5) | copy-start | bytes 3145732
  10.9 1.7 copy-start.1
  10.9 211.2 %all-gather.3.cloned.1.call-start = ((), (), s32[]{:S(2)}) async-start(), calls=%async_computation.1 | async-start | bytes 17825792 | tf_op jit(solution)/shard_map/all_gather | solution.py:21
Sparse Core Ops, SparseCore 0:
  11.0 88.8 all-gather.4
  102.0 120.0 all-gather.2
where the time goes:
time: 326 us; the launch traced here: 325 us
  waiting for transfers between devices  209 us (64%)
  blocking collectives  38.3 us (12%)
  local copies, waits for them, and re-layouts  23.4 us (7%)
  matrix products  22.4 us (7%)
  other arithmetic  18.4 us (6%)
  between operations  13.5 us (4%)
    all_gather x1, waiting for transfers between devices, local(): whole_left = lax.all_gather(masked_left, 'col', axis=1, tiled=True)  122 us
    all_gather x1, waiting for transfers between devices, local(): lax.all_gather(masked_right, 'row', axis=0, tiled=True)  87.2 us
    all_to_all x1, blocking collectives, local(): lax.all_to_all(pieces, ('row', 'col'), split_axis=0, concat_axis=0, tiled...  38.3 us
    dot_general x1, matrix products, local(): jnp.dot(whole_left, lax.all_gather(masked_right, 'row', axis=0, tiled=Tru...  22.4 us
    unnamed x9, local copies, waits for them, and re-layouts  15.3 us
    all_to_all x1, other arithmetic, local(): lax.all_to_all(pieces, ('row', 'col'), split_axis=0, concat_axis=0, tiled...  13.2 us
    all_to_all x2, local copies, waits for them, and re-layouts, local(): lax.all_to_all(pieces, ('row', 'col'), split_axis=0, concat_axis=0, tiled...  7.03 us
  transfers between devices with their start and end apart: 2, of which 2 were waited for; matrix products, arithmetic and copies ran while one was open for 0% of the time, Pallas kernels for 0%

commit v1 on v0

v1 whole, which is shorter than its diff:
```python
import jax
import jax.numpy as jnp
from jax import lax
from jax.experimental import pallas as pl
from jax.experimental.pallas import tpu as pltpu
from jax.sharding import PartitionSpec as P

TILE = 128
MESH = pl.DeviceIdType.MESH
F32 = jnp.float32
BF16 = jnp.bfloat16
SIDE = 4
MIB = 1 << 20


def wrap(value, size=SIDE):
    return lax.rem(value + size, size)


def contract(
    lm_ref,
    rm_ref,
    om_ref,
    left_ref,
    right_ref,
    out_ref,
    a_buf,
    b_buf,
    a_stage,
    b_stage,
    total,
    kept,
    load_sem,
    a_send,
    a_recv,
    b_send,
    b_recv,
    x_send,
    x_recv,
    own_sem,
):
    row = lax.axis_index("row")
    col = lax.axis_index("col")
    z = row // 2
    core = lax.rem(row, 2)
    y = col // SIDE
    x = lax.rem(col, SIDE)

    load_a = pltpu.make_async_copy(left_ref, a_stage, load_sem.at[0])
    load_b = pltpu.make_async_copy(right_ref, b_stage, load_sem.at[1])
    load_a.start()
    load_b.start()

    barrier = pltpu.get_barrier_semaphore()
    me = row * 16 + col

    def greet(step, carry):
        other = lax.rem(me + step, 128)
        pl.semaphore_signal(
            barrier,
            inc=1,
            device_id=(other // 16, lax.rem(other, 16)),
            device_id_type=MESH,
        )
        return carry

    lax.fori_loop(1, 128, greet, 0)

    x_off = pl.multiple_of(x * 512, 512)
    load_a.wait()
    for j in range(4):
        for i in range(8):
            keep = lm_ref[i, j].astype(F32)
            rows = slice(i * TILE, (i + 1) * TILE)
            block = a_stage[rows, j * TILE : (j + 1) * TILE].astype(F32) * keep
            a_buf[y, rows, pl.ds(pl.multiple_of(x_off + j * TILE, TILE), TILE)] = block.astype(BF16)
    load_b.wait()
    for i in range(8):
        rows = pl.ds(pl.multiple_of(core * 1024 + i * TILE, TILE), TILE)
        for j in range(8):
            keep = rm_ref[i, j].astype(F32)
            cols = slice(j * TILE, (j + 1) * TILE)
            block = b_stage[i * TILE : (i + 1) * TILE, cols].astype(F32) * keep
            b_buf[z, rows, cols] = block.astype(BF16)

    pl.semaphore_wait(barrier, 127)

    def at(dx, dy):
        return row, wrap(y + dy) * SIDE + wrap(x + dx)

    def a_piece(half, first, second, quarter):
        dx, dy = (first, second) if half == 0 else (second, first)
        start, size = half * 512, 512
        if quarter is not None:
            start, size = start + quarter * 256, 256
        cols = pl.ds(pl.multiple_of(wrap(x + dx) * 512, 512), 512)
        return a_buf.at[wrap(y + dy), pl.ds(start, size), cols]

    def a_slot(half, first, second, side):
        f_at = {0: 0, -1: 1, 1: 2, 2: 3}
        if second == 0:
            kind = {-1: 0, 1: 1, 2: 2}[first] + (1 if first == 2 and side == 1 else 0)
        else:
            kind = 4 + 4 * f_at[first] + {-1: 0, 1: 1, 2: 2}[second]
            kind += 1 if second == 2 and side == 1 else 0
        return half * 20 + kind

    a_sent = []

    def a_go(half, first, second, axis, step, quarter):
        if axis == 0:
            there = (first - step, second)
        else:
            there = (first, second - step)
        there = tuple(2 if abs(v) == 2 else v for v in there)
        slot = a_slot(half, *there, -step)
        along_x = (axis == 0) == (half == 0)
        device = at(step, 0) if along_x else at(0, step)
        piece = a_piece(half, first, second, quarter)
        copy = pltpu.make_async_remote_copy(
            src_ref=piece,
            dst_ref=piece,
            send_sem=a_send.at[slot],
            recv_sem=a_recv.at[slot],
            device_id=device,
            device_id_type=MESH,
        )
        copy.start()
        a_sent.append(copy)

    def a_wait(half, first, second, side=0):
        quarter = None
        if first == 2 and second == 0 or second == 2:
            quarter = 0 if side == -1 else 1
        piece = a_piece(half, first, second, quarter)
        slot = a_slot(half, first, second, side)
        pltpu.make_async_copy(piece, piece, a_recv.at[slot]).wait()

    def b_piece(dz, side, half):
        start = pl.multiple_of(side * 1024 + (0 if half is None else half * 512), 512)
        return b_buf.at[wrap(z + dz), pl.ds(start, 1024 if half is None else 512), :]

    b_sent = []

    def b_go(dz, half, step, slot):
        piece = b_piece(dz, core, half)
        device = (wrap(z + step) * 2 + core, col) if step else (z * 2 + 1 - core, col)
        copy = pltpu.make_async_remote_copy(
            src_ref=piece,
            dst_ref=piece,
            send_sem=b_send.at[slot],
            recv_sem=b_recv.at[slot],
            device_id=device,
            device_id_type=MESH,
        )
        copy.start()
        b_sent.append(copy)

    def b_wait(dz, half, slot, other=False):
        piece = b_piece(dz, 1 - core if other else core, half)
        pltpu.make_async_copy(piece, piece, b_recv.at[slot]).wait()

    halves = (0, 1)
    steps = (1, -1)
    for step in steps:
        for half in halves:
            a_go(half, 0, 0, 0, step, None)
    b_go(0, 0, 1, 0)
    b_go(0, 1, -1, 1)
    b_go(0, 1, 1, 2)
    b_go(0, 0, -1, 3)
    for step in steps:
        for half in halves:
            a_go(half, 0, 0, 1, step, None)
    b_go(0, None, 0, 6)

    for half in halves:
        a_wait(half, -1, 0)
        a_go(half, -1, 0, 0, 1, 0)
        a_wait(half, 1, 0)
        a_go(half, 1, 0, 0, -1, 1)
    for first in (-1, 1):
        for half in halves:
            for step in steps:
                a_go(half, first, 0, 1, step, None)

    def relay(first):
        for half in halves:
            a_wait(half, first, -1)
            a_go(half, first, -1, 1, 1, 0)
            a_wait(half, first, 1)
            a_go(half, first, 1, 1, -1, 1)

    relay(0)
    b_wait(-1, 0, 0)
    b_go(-1, 0, 1, 4)
    b_wait(1, 1, 1)
    b_go(1, 1, -1, 5)
    b_go(-1, 0, 0, 7)
    b_go(1, 1, 0, 8)
    for half in halves:
        a_wait(half, 2, 0, -1)
        a_wait(half, 2, 0, 1)
        for step in steps:
            a_go(half, 2, 0, 1, step, None)
    relay(-1)
    b_wait(-1, 1, 2)
    b_go(-1, 1, 0, 9)
    b_wait(1, 0, 3)
    b_go(1, 0, 0, 10)
    relay(1)
    relay(2)
    b_wait(2, 0, 4)
    b_go(2, 0, 0, 11)
    b_wait(2, 1, 5)
    b_go(2, 1, 0, 12)

    b_wait(0, None, 6, True)
    b_wait(-1, 0, 7, True)
    b_wait(1, 1, 8, True)
    b_wait(-1, 1, 9, True)
    b_wait(1, 0, 10, True)
    b_wait(2, 0, 11, True)
    b_wait(2, 1, 12, True)

    def a_end(half, first):
        a_wait(half, first, 2, -1)
        a_wait(half, first, 2, 1)

    def add(half, dy, fresh):
        group = wrap(y + dy)
        rows = pl.ds(half * 512, 512)

        def one(n, carry):
            cols = pl.ds(pl.multiple_of(n * 256, 256), 256)
            part = jnp.dot(a_buf[group, rows, :], b_buf[group, :, cols], preferred_element_type=F32)
            if fresh:
                total[rows, cols] = part
            else:
                total[rows, cols] += part
            return carry

        lax.fori_loop(0, 4, one, 0)

    add(0, 0, True)
    add(0, -1, False)
    add(0, 1, False)
    a_end(1, 0)
    add(1, 0, True)
    a_end(1, -1)
    add(1, -1, False)
    a_end(1, 1)
    add(1, 1, False)
    a_end(1, 2)
    for first in (0, -1, 1, 2):
        a_end(0, first)

    last = wrap(y + 2)
    order = (2, 1, 3, 0)

    def finish(dz):
        quarter = wrap(z + dz)
        rows = pl.ds(pl.multiple_of(quarter * 256, 256), 256)

        def one(n, carry):
            cols = pl.ds(pl.multiple_of(n * 256, 256), 256)
            part = total[rows, cols] + jnp.dot(
                a_buf[last, rows, :], b_buf[last, :, cols], preferred_element_type=F32
            )
            for i in range(2):
                for j in range(2):
                    keep = om_ref[quarter * 2 + i, n * 2 + j].astype(F32)
                    block = part[i * TILE : (i + 1) * TILE, j * TILE : (j + 1) * TILE] * keep
                    kept[
                        pl.ds(quarter * 32 + i * 16, 16),
                        :,
                        pl.ds(pl.multiple_of(n * 256 + j * TILE, TILE), TILE),
                    ] = block.reshape(16, 8, TILE).astype(BF16)
            return carry

        lax.fori_loop(0, 4, one, 0)

    def hand_out(dz):
        quarter = wrap(z + dz)

        def one(t, carry):
            to_core = lax.rem(core + t // 16, 2)
            to_y = wrap(y + lax.rem(t // 4, 4))
            to_x = wrap(x + lax.rem(t, 4))
            to_row = quarter * 2 + to_core
            to_col = to_y * 4 + to_x
            pltpu.make_async_remote_copy(
                src_ref=kept.at[to_row * 16 + to_col],
                dst_ref=out_ref.at[me],
                send_sem=x_send,
                recv_sem=x_recv,
                device_id=(to_row, to_col),
                device_id_type=MESH,
            ).start()
            return carry

        lax.fori_loop(1 if dz == 0 else 0, 32, one, 0)

    finish(order[0])
    for now, later in zip(order, order[1:]):
        finish(later)
        hand_out(now)
    hand_out(order[-1])
    own = pltpu.make_async_copy(kept.at[me], out_ref.at[me], own_sem)
    own.start()

    for copy in a_sent + b_sent:
        copy.wait_send()
    own.wait()
    pltpu.make_async_copy(kept.at[pl.ds(0, 127)], kept.at[pl.ds(0, 127)], x_send).wait()
    pltpu.make_async_copy(out_ref.at[pl.ds(0, 127)], out_ref.at[pl.ds(0, 127)], x_recv).wait()


def flatten_kernel(in_ref, out_ref):
    block = in_ref[...].astype(F32)
    turned = jnp.swapaxes(block, 0, 1)
    for a in range(8):
        out_ref[:, a * 1024 : (a + 1) * 1024] = turned[a].astype(BF16)


def local(left_amps, right_ints, left_mask, right_mask, result_mask):
    smem = pl.BlockSpec(memory_space=pltpu.SMEM)
    hbm = pl.BlockSpec(memory_space=pl.ANY)
    strips = pl.pallas_call(
        contract,
        out_shape=jax.ShapeDtypeStruct((128, 8, 1024), BF16),
        in_specs=[smem, smem, smem, hbm, hbm],
        out_specs=hbm,
        scratch_shapes=[
            pltpu.VMEM((4, 1024, 2048), BF16),
            pltpu.VMEM((4, 2048, 1024), BF16),
            pltpu.VMEM((1024, 512), BF16),
            pltpu.VMEM((1024, 1024), BF16),
            pltpu.VMEM((1024, 1024), F32),
            pltpu.VMEM((128, 8, 1024), BF16),
            pltpu.SemaphoreType.DMA((2,)),
            pltpu.SemaphoreType.DMA((40,)),
            pltpu.SemaphoreType.DMA((40,)),
            pltpu.SemaphoreType.DMA((13,)),
            pltpu.SemaphoreType.DMA((13,)),
            pltpu.SemaphoreType.DMA(()),
            pltpu.SemaphoreType.DMA(()),
            pltpu.SemaphoreType.DMA(()),
        ],
        compiler_params=pltpu.CompilerParams(
            collective_id=0, has_side_effects=True, vmem_limit_bytes=60 * MIB
        ),
        name="contract",
    )(left_mask, right_mask, result_mask, left_amps, right_ints)
    return pl.pallas_call(
        flatten_kernel,
        grid=(8,),
        in_specs=[pl.BlockSpec((16, 8, 1024), lambda p: (p, 0, 0))],
        out_specs=pl.BlockSpec((16, 8192), lambda p: (p, 0)),
        out_shape=jax.ShapeDtypeStruct((128, 8192), BF16),
        name="flatten",
    )(strips)


def solution(mesh):
    in_specs = (P("row", "col"), P("row", "col"), P("row", "col"), P("row", "col"), P("row", "col"))
    out_specs = P(None, ("row", "col"))
    return jax.shard_map(local, mesh=mesh, in_specs=in_specs, out_specs=out_specs, check_vma=False)
```

time: 326 us -> 152 us (0.47)
  waiting for transfers between devices: 209 us -> 0 us
  Pallas kernels: 0 us -> 150 us
  blocking collectives: 38.3 us -> 0 us
  matrix products: 22.4 us -> 0 us
  local copies, waits for them, and re-layouts: 23.4 us -> 1.35 us
  other arithmetic: 18.4 us -> 0 us
  between operations: 13.5 us -> 0.01 us
    all_gather x2 -> x0, waiting for transfers between devices: 209 us -> none  [the longest x1 122 us: local(): whole_left = lax.all_gather(masked_left, 'col', axis=1, tiled=True)]
    pallas_call x0 -> x2, Pallas kernels: none -> 150 us  [the longest x1 144 us: local(): pl.pallas_call(contract, out_shape=jax.ShapeDtypeStruct((128, 8, 1024), B...]
    all_to_all x1 -> x0, blocking collectives: 38.3 us -> none  [local(): lax.all_to_all(pieces, ('row', 'col'), split_axis=0, concat_axis=0, tiled...]
    dot_general x1 -> x0, matrix products: 22.4 us -> none  [local(): jnp.dot(whole_left, lax.all_gather(masked_right, 'row', axis=0, tiled=Tru...]
    unnamed x9 -> x1, local copies, waits for them, and re-layouts: 15.3 us -> 1.35 us
    all_to_all x1 -> x0, other arithmetic: 13.2 us -> none  [local(): lax.all_to_all(pieces, ('row', 'col'), split_axis=0, concat_axis=0, tiled...]
    all_to_all x2 -> x0, local copies, waits for them, and re-layouts: 7.03 us -> none  [local(): lax.all_to_all(pieces, ('row', 'col'), split_axis=0, concat_axis=0, tiled...]
    mul x2 -> x0, other arithmetic: 4.43 us -> none  [expand(): kept = tiled * mask.astype(values.dtype)[:, None, :, None]]
  transfers between devices with their start and end apart: 2 -> 0, of which waited for: 2 -> 0; matrix products, arithmetic and copies ran while one was open for 0% -> 0% of each run, Pallas kernels for 0% -> 0%
where the time goes in v1:
time: 152 us; the launch traced here: 151 us
  Pallas kernels  150 us (99%)
    pallas_call x1, Pallas kernels, local(): pl.pallas_call(contract, out_shape=jax.ShapeDtypeStruct((128, 8, 1024), B...  144 us
    pallas_call x1, Pallas kernels, local(): pl.pallas_call(flatten_kernel, grid=(8,), in_specs=[pl.BlockSpec((16, 8,...  6.05 us

profile of v1, /device:TPU:1, one launch (start us, length us, event | category | flops | bytes accessed | tf_op | source)
XLA Modules:
  0.0 151.3 jit_solution(16950568669033043351)
XLA Ops:
  0.0 1.3 copy.6.lm_ref
  1.3 143.9 %contract.1.in_ref = bf16[128,8,1024]{2,1,0:T(8,128)(2,1)} custom-call(s32[8,4]{1,0:T(8,128)} %copy.6.lm_ref, s32[8,8]{1,0:T(8,128)} %rm_ref.1, s32[8,8]{1,0:T(8,128)} %om_ref.1, bf16[1024,512]{1,0:T(8,128)(2,1)} %left_ref.1, bf16[1024,1024]{1,0:T(8,128)(2,1)} %right_ref.1), custom_call_target="tpu_custom_call" | custom-call | tf_op jit(solution)/shard_map/contract/pallas_call | solution.py:329
  145.2 6.0 %flatten.1 = bf16[128,8192]{1,0:T(8,128)(2,1)} custom-call(bf16[128,8,1024]{2,1,0:T(8,128)(2,1)} %contract.1.in_ref), custom_call_target="tpu_custom_call" | custom-call | tf_op jit(solution)/shard_map/flatten/pallas_call | solution.py:355

commit v2 on v1

--- a/solution.py
+++ b/solution.py
@@ -38,6 +38,7 @@
     x_send,
     x_recv,
     own_sem,
+    round_sem,
 ):
     row = lax.axis_index("row")
     col = lax.axis_index("col")
@@ -54,23 +55,28 @@
     barrier = pltpu.get_barrier_semaphore()
     me = row * 16 + col
 
-    def greet(step, carry):
-        other = lax.rem(me + step, 128)
-        pl.semaphore_signal(
-            barrier,
-            inc=1,
-            device_id=(other // 16, lax.rem(other, 16)),
-            device_id_type=MESH,
-        )
-        return carry
-
-    lax.fori_loop(1, 128, greet, 0)
+    def at(dx, dy):
+        return row, wrap(y + dy) * SIDE + wrap(x + dx)
+
+    def along_z(step):
+        return wrap(z + step) * 2 + core, col
+
+    x_side = (at(1, 0), at(-1, 0))
+    y_side = (at(0, 1), at(0, -1))
+    z_side = (along_z(1), along_z(-1))
+    mate = (z * 2 + 1 - core, col)
+
+    def greet(sem, devices):
+        for device in devices:
+            pl.semaphore_signal(sem, inc=1, device_id=device, device_id_type=MESH)
+
+    greet(barrier, (*x_side, *y_side, *z_side, mate))
 
     x_off = pl.multiple_of(x * 512, 512)
     load_a.wait()
     for j in range(4):
         for i in range(8):
-            keep = lm_ref[i, j].astype(F32)
+            keep = lm_ref[j, i].astype(F32)
             rows = slice(i * TILE, (i + 1) * TILE)
             block = a_stage[rows, j * TILE : (j + 1) * TILE].astype(F32) * keep
             a_buf[y, rows, pl.ds(pl.multiple_of(x_off + j * TILE, TILE), TILE)] = block.astype(BF16)
@@ -83,10 +89,16 @@
             block = b_stage[i * TILE : (i + 1) * TILE, cols].astype(F32) * keep
             b_buf[z, rows, cols] = block.astype(BF16)
 
-    pl.semaphore_wait(barrier, 127)
-
-    def at(dx, dy):
-        return row, wrap(y + dy) * SIDE + wrap(x + dx)
+    pl.semaphore_wait(barrier, 7)
+
+    rounds = (x_side, y_side, y_side, z_side, z_side, (mate,))
+
+    def pass_on(step):
+        if step > 0:
+            pl.semaphore_wait(round_sem.at[step - 1], len(rounds[step - 1]))
+        if step < len(rounds):
+            greet(round_sem.at[step], rounds[step])
+
 
     def a_piece(half, first, second, quarter):
         dx, dy = (first, second) if half == 0 else (second, first)
@@ -136,43 +148,81 @@
         slot = a_slot(half, first, second, side)
         pltpu.make_async_copy(piece, piece, a_recv.at[slot]).wait()
 
-    def b_piece(dz, side, half):
-        start = pl.multiple_of(side * 1024 + (0 if half is None else half * 512), 512)
-        return b_buf.at[wrap(z + dz), pl.ds(start, 1024 if half is None else 512), :]
-
-    b_sent = []
-
-    def b_go(dz, half, step, slot):
-        piece = b_piece(dz, core, half)
+    def a_end(half, first):
+        a_wait(half, first, 2, -1)
+        a_wait(half, first, 2, 1)
+
+    near = wrap(y - z)
+
+    def b_piece(dz, side, piece, count=1):
+        start = pl.multiple_of(side * 1024 + piece * 256, 256)
+        return b_buf.at[wrap(z + dz), pl.ds(start, 256 * count), :]
+
+    def b_go(dz, piece, step, count=1):
+        if step and dz == 0:
+            slot = piece + (0 if step == 1 else 4)
+        elif step:
+            slot = 8 + piece
+        else:
+            slot = {0: 12, -1: 13, 1: 17, 2: 21}[dz] + piece
+        part = b_piece(dz, core, piece, count)
         device = (wrap(z + step) * 2 + core, col) if step else (z * 2 + 1 - core, col)
-        copy = pltpu.make_async_remote_copy(
-            src_ref=piece,
-            dst_ref=piece,
+        pltpu.make_async_remote_copy(
+            src_ref=part,
+            dst_ref=part,
             send_sem=b_send.at[slot],
             recv_sem=b_recv.at[slot],
             device_id=device,
             device_id_type=MESH,
-        )
-        copy.start()
-        b_sent.append(copy)
-
-    def b_wait(dz, half, slot, other=False):
-        piece = b_piece(dz, 1 - core if other else core, half)
-        pltpu.make_async_copy(piece, piece, b_recv.at[slot]).wait()
+        ).start()
+
+    def b_wait(dz, piece, other=False, count=1):
+        if other:
+            slot = {0: 12, -1: 13, 1: 17, 2: 21}[dz] + piece
+        else:
+            slot = {-1: 0, 1: 4, 2: 8}[dz] + piece
+        part = b_piece(dz, 1 - core if other else core, piece, count)
+        pltpu.make_async_copy(part, part, b_recv.at[slot]).wait()
+
+    def b_relay(dz, piece):
+        b_wait(dz, piece)
+        b_go(dz, piece, -dz)
+        b_go(dz, piece, 0)
+
+    def b_rest(dz):
+        for piece in {0: (), -1: (2, 3), 1: (1, 0), 2: (0, 3, 1, 2)}[dz]:
+            b_wait(dz, piece)
+            b_go(dz, piece, 0)
+        if dz == 0:
+            b_wait(0, 0, True, 4)
+        else:
+            for piece in range(4):
+                b_wait(dz, piece, True)
+
+    up, down = (0, 1, 2, 3), (3, 2, 1, 0)
+
+    def own_up():
+        for piece in up[1:]:
+            b_go(0, piece, 1)
+
+    def own_down():
+        for piece in down[1:]:
+            b_go(0, piece, -1)
 
     halves = (0, 1)
     steps = (1, -1)
     for step in steps:
         for half in halves:
             a_go(half, 0, 0, 0, step, None)
-    b_go(0, 0, 1, 0)
-    b_go(0, 1, -1, 1)
-    b_go(0, 1, 1, 2)
-    b_go(0, 0, -1, 3)
+    b_go(0, up[0], 1)
+    b_go(0, down[0], -1)
+    pl.when(near != 3)(own_up)
+    pl.when(near != 1)(own_down)
     for step in steps:
         for half in halves:
             a_go(half, 0, 0, 1, step, None)
-    b_go(0, None, 0, 6)
+    b_go(0, 0, 0, 4)
+    pass_on(0)
 
     for half in halves:
         a_wait(half, -1, 0)
@@ -183,6 +233,10 @@
         for half in halves:
             for step in steps:
                 a_go(half, first, 0, 1, step, None)
+    pass_on(1)
+    b_relay(-1, 0)
+    b_relay(1, 3)
+    pass_on(2)
 
     def relay(first):
         for half in halves:
@@ -192,40 +246,26 @@
             a_go(half, first, 1, 1, -1, 1)
 
     relay(0)
-    b_wait(-1, 0, 0)
-    b_go(-1, 0, 1, 4)
-    b_wait(1, 1, 1)
-    b_go(1, 1, -1, 5)
-    b_go(-1, 0, 0, 7)
-    b_go(1, 1, 0, 8)
+
+    def second_relays():
+        b_relay(-1, 1)
+        b_relay(1, 2)
+
+    pl.when(near != 2)(second_relays)
+    pl.when(near == 3)(own_up)
+    pl.when(near == 1)(own_down)
+    pass_on(3)
     for half in halves:
         a_wait(half, 2, 0, -1)
         a_wait(half, 2, 0, 1)
         for step in steps:
             a_go(half, 2, 0, 1, step, None)
+    pass_on(4)
     relay(-1)
-    b_wait(-1, 1, 2)
-    b_go(-1, 1, 0, 9)
-    b_wait(1, 0, 3)
-    b_go(1, 0, 0, 10)
-    relay(1)
-    relay(2)
-    b_wait(2, 0, 4)
-    b_go(2, 0, 0, 11)
-    b_wait(2, 1, 5)
-    b_go(2, 1, 0, 12)
-
-    b_wait(0, None, 6, True)
-    b_wait(-1, 0, 7, True)
-    b_wait(1, 1, 8, True)
-    b_wait(-1, 1, 9, True)
-    b_wait(1, 0, 10, True)
-    b_wait(2, 0, 11, True)
-    b_wait(2, 1, 12, True)
-
-    def a_end(half, first):
-        a_wait(half, first, 2, -1)
-        a_wait(half, first, 2, 1)
+    pass_on(5)
+    pl.when(near == 2)(second_relays)
+    for dz in (0, 1, 2, -1):
+        pl.when(near == dz % SIDE)(lambda dz=dz: b_rest(dz))
 
     def add(half, dy, fresh):
         group = wrap(y + dy)
@@ -243,52 +283,62 @@
         lax.fori_loop(0, 4, one, 0)
 
     add(0, 0, True)
-    add(0, -1, False)
-    add(0, 1, False)
+    relay(1)
+    pass_on(6)
     a_end(1, 0)
     add(1, 0, True)
+    relay(2)
+    for dz in (0, 1, -1, 2):
+        pl.when(near != dz % SIDE)(lambda dz=dz: b_rest(dz))
+
+    add(0, -1, False)
     a_end(1, -1)
     add(1, -1, False)
     a_end(1, 1)
-    add(1, 1, False)
     a_end(1, 2)
     for first in (0, -1, 1, 2):
         a_end(0, first)
 
-    last = wrap(y + 2)
-    order = (2, 1, 3, 0)
-
-    def finish(dz):
-        quarter = wrap(z + dz)
-        rows = pl.ds(pl.multiple_of(quarter * 256, 256), 256)
+    order = (0, 1, 3, 2)
+
+    def strips_of(part):
+        found = []
+        for dz in range(SIDE):
+            there_y = wrap(y + (part - dz) % SIDE)
+            for there_core in range(2):
+                found.append((wrap(z + dz) * 2 + there_core, there_y))
+        return found
+
+    def finish(part):
+        strips = strips_of(part)
+        rows = [pl.ds(pl.multiple_of(g * TILE + v * 32, 32), 32) for g, v in strips]
 
         def one(n, carry):
             cols = pl.ds(pl.multiple_of(n * 256, 256), 256)
-            part = total[rows, cols] + jnp.dot(
-                a_buf[last, rows, :], b_buf[last, :, cols], preferred_element_type=F32
-            )
-            for i in range(2):
+            value = jnp.concatenate([total[r, cols] for r in rows], axis=0)
+            for dy in (1, 2):
+                group = wrap(y + dy)
+                lhs = jnp.concatenate([a_buf[group, r, :] for r in rows], axis=0)
+                value += jnp.dot(lhs, b_buf[group, :, cols], preferred_element_type=F32)
+            for i, (g, v) in enumerate(strips):
                 for j in range(2):
-                    keep = om_ref[quarter * 2 + i, n * 2 + j].astype(F32)
-                    block = part[i * TILE : (i + 1) * TILE, j * TILE : (j + 1) * TILE] * keep
+                    keep = om_ref[g, n * 2 + j].astype(F32)
+                    block = value[i * 32 : (i + 1) * 32, j * TILE : (j + 1) * TILE] * keep
                     kept[
-                        pl.ds(quarter * 32 + i * 16, 16),
+                        pl.ds(g * 16 + v * 4, 4),
                         :,
                         pl.ds(pl.multiple_of(n * 256 + j * TILE, TILE), TILE),
-                    ] = block.reshape(16, 8, TILE).astype(BF16)
+                    ] = block.reshape(4, 8, TILE).astype(BF16)
             return carry
 
         lax.fori_loop(0, 4, one, 0)
 
-    def hand_out(dz):
-        quarter = wrap(z + dz)
-
+    def hand_out(part):
         def one(t, carry):
-            to_core = lax.rem(core + t // 16, 2)
-            to_y = wrap(y + lax.rem(t // 4, 4))
-            to_x = wrap(x + lax.rem(t, 4))
-            to_row = quarter * 2 + to_core
-            to_col = to_y * 4 + to_x
+            dz = lax.rem(t, 4)
+            to_row = wrap(z + dz) * 2 + lax.rem(core + t // 16, 2)
+            to_y = lax.rem(y + part + 4 - dz, 4)
+            to_col = to_y * 4 + lax.rem(x + t + t // 4, 4)
             pltpu.make_async_remote_copy(
                 src_ref=kept.at[to_row * 16 + to_col],
                 dst_ref=out_ref.at[me],
@@ -299,7 +349,7 @@
             ).start()
             return carry
 
-        lax.fori_loop(1 if dz == 0 else 0, 32, one, 0)
+        lax.fori_loop(1 if part == 0 else 0, 32, one, 0)
 
     finish(order[0])
     for now, later in zip(order, order[1:]):
@@ -309,18 +359,18 @@
     own = pltpu.make_async_copy(kept.at[me], out_ref.at[me], own_sem)
     own.start()
 
-    for copy in a_sent + b_sent:
+    for copy in a_sent:
         copy.wait_send()
+    for slot in range(25):
+        part = b_piece(0, core, 0, 4 if slot == 12 else 1)
+        pltpu.make_async_copy(part, part, b_send.at[slot]).wait()
     own.wait()
     pltpu.make_async_copy(kept.at[pl.ds(0, 127)], kept.at[pl.ds(0, 127)], x_send).wait()
     pltpu.make_async_copy(out_ref.at[pl.ds(0, 127)], out_ref.at[pl.ds(0, 127)], x_recv).wait()
 
 
 def flatten_kernel(in_ref, out_ref):
-    block = in_ref[...].astype(F32)
-    turned = jnp.swapaxes(block, 0, 1)
-    for a in range(8):
-        out_ref[:, a * 1024 : (a + 1) * 1024] = turned[a].astype(BF16)
+    out_ref[...] = in_ref[...].reshape(out_ref.shape)
 
 
 def local(left_amps, right_ints, left_mask, right_mask, result_mask):
@@ -341,22 +391,23 @@
             pltpu.SemaphoreType.DMA((2,)),
             pltpu.SemaphoreType.DMA((40,)),
             pltpu.SemaphoreType.DMA((40,)),
-            pltpu.SemaphoreType.DMA((13,)),
-            pltpu.SemaphoreType.DMA((13,)),
+            pltpu.SemaphoreType.DMA((25,)),
+            pltpu.SemaphoreType.DMA((25,)),
             pltpu.SemaphoreType.DMA(()),
             pltpu.SemaphoreType.DMA(()),
             pltpu.SemaphoreType.DMA(()),
+            pltpu.SemaphoreType.REGULAR((6,)),
         ],
         compiler_params=pltpu.CompilerParams(
             collective_id=0, has_side_effects=True, vmem_limit_bytes=60 * MIB
         ),
         name="contract",
-    )(left_mask, right_mask, result_mask, left_amps, right_ints)
+    )(left_mask.T, right_mask, result_mask, left_amps, right_ints)
     return pl.pallas_call(
         flatten_kernel,
-        grid=(8,),
-        in_specs=[pl.BlockSpec((16, 8, 1024), lambda p: (p, 0, 0))],
-        out_specs=pl.BlockSpec((16, 8192), lambda p: (p, 0)),
+        grid=(2,),
+        in_specs=[pl.BlockSpec((64, 8, 1024), lambda p: (p, 0, 0))],
+        out_specs=pl.BlockSpec((64, 8192), lambda p: (p, 0)),
         out_shape=jax.ShapeDtypeStruct((128, 8192), BF16),
         name="flatten",
     )(strips)

time: 152 us -> 132 us (0.87)
  Pallas kernels: 150 us -> 131 us
    pallas_call x1, Pallas kernels: 144 us -> 129 us  [local(): pl.pallas_call(contract, out_shape=jax.ShapeDtypeStruct((128, 8, 1024), B...]
    pallas_call x1, Pallas kernels: 6.05 us -> 2.8 us  [local(): pl.pallas_call(flatten_kernel, grid=(2,), in_specs=[pl.BlockSpec((64, 8,...]
where the time goes in v2:
time: 132 us; the launch traced here: 131 us
  Pallas kernels  131 us (99%)
    pallas_call x1, Pallas kernels, local(): pl.pallas_call(contract, out_shape=jax.ShapeDtypeStruct((128, 8, 1024), B...  129 us
    pallas_call x1, Pallas kernels, local(): pl.pallas_call(flatten_kernel, grid=(2,), in_specs=[pl.BlockSpec((64, 8,...  2.8 us

profile of v2, /device:TPU:1, one launch (start us, length us, event | category | flops | bytes accessed | tf_op | source)
XLA Modules:
  0.0 131.3 jit_solution(16970499020866743415)
XLA Ops:
  0.0 128.5 %contract.1.in_ref = bf16[128,8,1024]{2,1,0:T(8,128)(2,1)} custom-call(s32[4,8]{1,0:T(4,128)} %bitcast.1, s32[8,8]{1,0:T(8,128)} %rm_ref.1, s32[8,8]{1,0:T(8,128)} %om_ref.1, bf16[1024,512]{1,0:T(8,128)(2,1)} %left_ref.1, bf16[1024,1024]{1,0:T(8,128)(2,1)} %right_ref.1), custom_call_target="tpu_custom_call" | custom-call | tf_op jit(solution)/shard_map/contract/pallas_call | solution.py:379
  128.5 2.8 %flatten.1 = bf16[128,8192]{1,0:T(8,128)(2,1)} custom-call(bf16[128,8,1024]{2,1,0:T(8,128)(2,1)} %contract.1.in_ref), custom_call_target="tpu_custom_call" | custom-call | tf_op jit(solution)/shard_map/flatten/pallas_call | solution.py:406

commit v3 on v2

--- a/solution.py
+++ b/solution.py
@@ -267,37 +267,49 @@
     for dz in (0, 1, 2, -1):
         pl.when(near == dz % SIDE)(lambda dz=dz: b_rest(dz))
 
-    def add(half, dy, fresh):
-        group = wrap(y + dy)
+    def depth(dx):
+        return pl.ds(pl.multiple_of(wrap(x + dx) * 512, 512), 512)
+
+    def add(half, blocks, fresh=False):
         rows = pl.ds(half * 512, 512)
+        width = 512 if blocks[0][1] is None else 1024
 
         def one(n, carry):
-            cols = pl.ds(pl.multiple_of(n * 256, 256), 256)
-            part = jnp.dot(a_buf[group, rows, :], b_buf[group, :, cols], preferred_element_type=F32)
+            cols = pl.ds(pl.multiple_of(n * width, width), width)
+            part = None
+            for dy, dx in blocks:
+                group, k = wrap(y + dy), slice(None) if dx is None else depth(dx)
+                term = jnp.dot(a_buf[group, rows, k], b_buf[group, k, cols], preferred_element_type=F32)
+                part = term if part is None else part + term
             if fresh:
                 total[rows, cols] = part
             else:
                 total[rows, cols] += part
             return carry
 
-        lax.fori_loop(0, 4, one, 0)
-
-    add(0, 0, True)
+        lax.fori_loop(0, 1024 // width, one, 0)
+
+    close = (0, -1, 1)
+    add(0, [(0, None)], True)
     relay(1)
     pass_on(6)
     a_end(1, 0)
-    add(1, 0, True)
-    relay(2)
+    add(1, [(0, None)], True)
     for dz in (0, 1, -1, 2):
         pl.when(near != dz % SIDE)(lambda dz=dz: b_rest(dz))
-
-    add(0, -1, False)
+    for dy in (-1, 1):
+        for half in halves:
+            add(half, [(dy, dx) for dx in close])
+    relay(2)
+    add(1, [(2, dx) for dx in close])
+    for first in close:
+        a_end(0, first)
+    add(0, [(2, dx) for dx in close] + [(-1, 2), (1, 2)])
     a_end(1, -1)
-    add(1, -1, False)
     a_end(1, 1)
+    add(1, [(-1, 2), (1, 2)])
     a_end(1, 2)
-    for first in (0, -1, 1, 2):
-        a_end(0, first)
+    a_end(0, 2)
 
     order = (0, 1, 3, 2)
 
@@ -312,26 +324,18 @@
     def finish(part):
         strips = strips_of(part)
         rows = [pl.ds(pl.multiple_of(g * TILE + v * 32, 32), 32) for g, v in strips]
-
-        def one(n, carry):
-            cols = pl.ds(pl.multiple_of(n * 256, 256), 256)
-            value = jnp.concatenate([total[r, cols] for r in rows], axis=0)
-            for dy in (1, 2):
-                group = wrap(y + dy)
-                lhs = jnp.concatenate([a_buf[group, r, :] for r in rows], axis=0)
-                value += jnp.dot(lhs, b_buf[group, :, cols], preferred_element_type=F32)
-            for i, (g, v) in enumerate(strips):
-                for j in range(2):
-                    keep = om_ref[g, n * 2 + j].astype(F32)
-                    block = value[i * 32 : (i + 1) * 32, j * TILE : (j + 1) * TILE] * keep
-                    kept[
-                        pl.ds(g * 16 + v * 4, 4),
-                        :,
-                        pl.ds(pl.multiple_of(n * 256 + j * TILE, TILE), TILE),
-                    ] = block.reshape(4, 8, TILE).astype(BF16)
-            return carry
-
-        lax.fori_loop(0, 4, one, 0)
+        group, k = wrap(y + 2), depth(2)
+
+        value = jnp.concatenate([total[r, :] for r in rows], axis=0)
+        lhs = jnp.concatenate([a_buf[group, r, k] for r in rows], axis=0)
+        value += jnp.dot(lhs, b_buf[group, k, :], preferred_element_type=F32)
+        for i, (g, v) in enumerate(strips):
+            for j in range(8):
+                keep = om_ref[g, j].astype(F32)
+                block = value[i * 32 : (i + 1) * 32, j * TILE : (j + 1) * TILE] * keep
+                kept[pl.ds(g * 16 + v * 4, 4), :, j * TILE : (j + 1) * TILE] = block.reshape(
+                    4, 8, TILE
+                ).astype(BF16)
 
     def hand_out(part):
         def one(t, carry):

time: 132 us -> 127 us (0.962)
  Pallas kernels: 131 us -> 127 us
    pallas_call x1, Pallas kernels: 129 us -> 124 us  [local(): pl.pallas_call(contract, out_shape=jax.ShapeDtypeStruct((128, 8, 1024), B...]
where the time goes in v3:
time: 127 us
  Pallas kernels  127 us (100%)
    pallas_call x1, Pallas kernels, local(): pl.pallas_call(contract, out_shape=jax.ShapeDtypeStruct((128, 8, 1024), B...  124 us
    pallas_call x1, Pallas kernels, local(): pl.pallas_call(flatten_kernel, grid=(2,), in_specs=[pl.BlockSpec((64, 8,...  2.8 us

profile of v3, /device:TPU:1, one launch (start us, length us, event | category | flops | bytes accessed | tf_op | source)
XLA Modules:
  0.0 127.1 jit_solution(5359059539333957253)
XLA Ops:
  0.0 124.3 %contract.1.in_ref = bf16[128,8,1024]{2,1,0:T(8,128)(2,1)} custom-call(s32[4,8]{1,0:T(4,128)} %bitcast.1, s32[8,8]{1,0:T(8,128)} %rm_ref.1, s32[8,8]{1,0:T(8,128)} %om_ref.1, bf16[1024,512]{1,0:T(8,128)(2,1)} %left_ref.1, bf16[1024,1024]{1,0:T(8,128)(2,1)} %right_ref.1), custom_call_target="tpu_custom_call" | custom-call | tf_op jit(solution)/shard_map/contract/pallas_call | solution.py:383
  124.3 2.8 %flatten.1 = bf16[128,8192]{1,0:T(8,128)(2,1)} custom-call(bf16[128,8,1024]{2,1,0:T(8,128)(2,1)} %contract.1.in_ref), custom_call_target="tpu_custom_call" | custom-call | tf_op jit(solution)/shard_map/flatten/pallas_call | solution.py:410

commit v4 on v3

--- a/solution.py
+++ b/solution.py
@@ -117,7 +117,7 @@
             kind += 1 if second == 2 and side == 1 else 0
         return half * 20 + kind
 
-    a_sent = []
+    a_sent = {}
 
     def a_go(half, first, second, axis, step, quarter):
         if axis == 0:
@@ -138,7 +138,7 @@
             device_id_type=MESH,
         )
         copy.start()
-        a_sent.append(copy)
+        a_sent[slot] = copy
 
     def a_wait(half, first, second, side=0):
         quarter = None
@@ -199,78 +199,10 @@
             for piece in range(4):
                 b_wait(dz, piece, True)
 
-    up, down = (0, 1, 2, 3), (3, 2, 1, 0)
-
-    def own_up():
-        for piece in up[1:]:
-            b_go(0, piece, 1)
-
-    def own_down():
-        for piece in down[1:]:
-            b_go(0, piece, -1)
-
-    halves = (0, 1)
-    steps = (1, -1)
-    for step in steps:
-        for half in halves:
-            a_go(half, 0, 0, 0, step, None)
-    b_go(0, up[0], 1)
-    b_go(0, down[0], -1)
-    pl.when(near != 3)(own_up)
-    pl.when(near != 1)(own_down)
-    for step in steps:
-        for half in halves:
-            a_go(half, 0, 0, 1, step, None)
-    b_go(0, 0, 0, 4)
-    pass_on(0)
-
-    for half in halves:
-        a_wait(half, -1, 0)
-        a_go(half, -1, 0, 0, 1, 0)
-        a_wait(half, 1, 0)
-        a_go(half, 1, 0, 0, -1, 1)
-    for first in (-1, 1):
-        for half in halves:
-            for step in steps:
-                a_go(half, first, 0, 1, step, None)
-    pass_on(1)
-    b_relay(-1, 0)
-    b_relay(1, 3)
-    pass_on(2)
-
-    def relay(first):
-        for half in halves:
-            a_wait(half, first, -1)
-            a_go(half, first, -1, 1, 1, 0)
-            a_wait(half, first, 1)
-            a_go(half, first, 1, 1, -1, 1)
-
-    relay(0)
-
-    def second_relays():
-        b_relay(-1, 1)
-        b_relay(1, 2)
-
-    pl.when(near != 2)(second_relays)
-    pl.when(near == 3)(own_up)
-    pl.when(near == 1)(own_down)
-    pass_on(3)
-    for half in halves:
-        a_wait(half, 2, 0, -1)
-        a_wait(half, 2, 0, 1)
-        for step in steps:
-            a_go(half, 2, 0, 1, step, None)
-    pass_on(4)
-    relay(-1)
-    pass_on(5)
-    pl.when(near == 2)(second_relays)
-    for dz in (0, 1, 2, -1):
-        pl.when(near == dz % SIDE)(lambda dz=dz: b_rest(dz))
-
     def depth(dx):
         return pl.ds(pl.multiple_of(wrap(x + dx) * 512, 512), 512)
 
-    def add(half, blocks, fresh=False):
+    def add(half, blocks):
         rows = pl.ds(half * 512, 512)
         width = 512 if blocks[0][1] is None else 1024
 
@@ -281,30 +213,109 @@
                 group, k = wrap(y + dy), slice(None) if dx is None else depth(dx)
                 term = jnp.dot(a_buf[group, rows, k], b_buf[group, k, cols], preferred_element_type=F32)
                 part = term if part is None else part + term
-            if fresh:
-                total[rows, cols] = part
-            else:
-                total[rows, cols] += part
+            total[rows, cols] += part
             return carry
 
         lax.fori_loop(0, 1024 // width, one, 0)
 
+    halves = (0, 1)
+    steps = (1, -1)
     close = (0, -1, 1)
-    add(0, [(0, None)], True)
-    relay(1)
+    for step in steps:
+        for half in halves:
+            a_go(half, 0, 0, 0, step, None)
+    for piece in (0, 1):
+        b_go(0, piece, 1)
+        b_go(0, 3 - piece, -1)
+    for step in steps:
+        for half in halves:
+            a_go(half, 0, 0, 1, step, None)
+    b_go(0, 0, 0, 4)
+    pass_on(0)
+    total[...] = jnp.zeros_like(total)
+
+    for half in halves:
+        a_wait(half, -1, 0)
+        a_go(half, -1, 0, 0, 1, 0)
+        a_wait(half, 1, 0)
+        a_go(half, 1, 0, 0, -1, 1)
+    for first in (-1, 1):
+        for half in halves:
+            for step in steps:
+                a_go(half, first, 0, 1, step, None)
+    for piece in (2, 3):
+        b_go(0, piece, 1)
+        b_go(0, 3 - piece, -1)
+    pass_on(1)
+
+    def arrived(first):
+        for half in halves:
+            a_wait(half, first, -1)
+            a_wait(half, first, 1)
+
+    def relay(first):
+        for half in halves:
+            a_go(half, first, -1, 1, 1, 0)
+            a_go(half, first, 1, 1, -1, 1)
+
+    def gone(first):
+        for half in halves:
+            for side in steps:
+                a_sent.pop(a_slot(half, first, side, side)).wait_send()
+
+    arrived(0)
+    relay(0)
+    pass_on(2)
+    for half in halves:
+        a_wait(half, 2, 0, -1)
+        a_wait(half, 2, 0, 1)
+        for step in steps:
+            a_go(half, 2, 0, 1, step, None)
+    pass_on(3)
+    for piece in (0, 1):
+        b_relay(-1, piece)
+        b_relay(1, 3 - piece)
+    pass_on(4)
+    for dz in (0, 1, -1):
+        b_rest(dz)
+    pass_on(5)
+
+    def in_time(half, dy, dx):
+        pl.when(near != (2 - dy) % SIDE)(lambda: add(half, dx(dy)))
+
+    def late(half, dy, dx):
+        pl.when(near == (2 - dy) % SIDE)(lambda: add(half, dx(dy)))
+
+    def whole_row(dy):
+        return [(dy, None)]
+
+    def three(dy):
+        return [(dy, dx) for dx in close]
+
+    in_time(0, 0, whole_row)
+    gone(-1)
+    arrived(-1)
+    relay(-1)
     pass_on(6)
     a_end(1, 0)
-    add(1, [(0, None)], True)
-    for dz in (0, 1, -1, 2):
-        pl.when(near != dz % SIDE)(lambda dz=dz: b_rest(dz))
-    for dy in (-1, 1):
-        for half in halves:
-            add(half, [(dy, dx) for dx in close])
+    in_time(1, 0, whole_row)
+    arrived(1)
+    for half in halves:
+        for dy in (-1, 1):
+            in_time(half, dy, three)
+    gone(2)
+    relay(1)
+    arrived(2)
     relay(2)
-    add(1, [(2, dx) for dx in close])
+    b_rest(2)
+    for half in halves:
+        late(half, 0, whole_row)
+        for dy in (-1, 1):
+            late(half, dy, three)
+    add(1, three(2))
     for first in close:
         a_end(0, first)
-    add(0, [(2, dx) for dx in close] + [(-1, 2), (1, 2)])
+    add(0, three(2) + [(-1, 2), (1, 2)])
     a_end(1, -1)
     a_end(1, 1)
     add(1, [(-1, 2), (1, 2)])
@@ -363,7 +374,7 @@
     own = pltpu.make_async_copy(kept.at[me], out_ref.at[me], own_sem)
     own.start()
 
-    for copy in a_sent:
+    for copy in a_sent.values():
         copy.wait_send()
     for slot in range(25):
         part = b_piece(0, core, 0, 4 if slot == 12 else 1)

time: 127 us -> 126 us (level)
  no operation moved by 1% of the time
where the time goes in v4:
time: 126 us
  Pallas kernels  126 us (100%)
    pallas_call x1, Pallas kernels, local(): pl.pallas_call(contract, out_shape=jax.ShapeDtypeStruct((128, 8, 1024), B...  123 us
    pallas_call x1, Pallas kernels, local(): pl.pallas_call(flatten_kernel, grid=(2,), in_specs=[pl.BlockSpec((64, 8,...  2.8 us

profile of v4, /device:TPU:1, one launch (start us, length us, event | category | flops | bytes accessed | tf_op | source)
XLA Modules:
  0.0 126.1 jit_solution(4288919623346999345)
XLA Ops:
  0.0 123.3 %contract.1.in_ref = bf16[128,8,1024]{2,1,0:T(8,128)(2,1)} custom-call(s32[4,8]{1,0:T(4,128)} %bitcast.1, s32[8,8]{1,0:T(8,128)} %rm_ref.1, s32[8,8]{1,0:T(8,128)} %om_ref.1, bf16[1024,512]{1,0:T(8,128)(2,1)} %left_ref.1, bf16[1024,1024]{1,0:T(8,128)(2,1)} %right_ref.1), custom_call_target="tpu_custom_call" | custom-call | tf_op jit(solution)/shard_map/contract/pallas_call | solution.py:394
  123.3 2.8 %flatten.1 = bf16[128,8192]{1,0:T(8,128)(2,1)} custom-call(bf16[128,8,1024]{2,1,0:T(8,128)(2,1)} %contract.1.in_ref), custom_call_target="tpu_custom_call" | custom-call | tf_op jit(solution)/shard_map/flatten/pallas_call | solution.py:421

commit v5 on v4

--- a/solution.py
+++ b/solution.py
@@ -18,9 +18,9 @@
 
 
 def contract(
-    lm_ref,
-    rm_ref,
-    om_ref,
+    lm_hbm,
+    rm_hbm,
+    om_hbm,
     left_ref,
     right_ref,
     out_ref,
@@ -39,6 +39,9 @@
     x_recv,
     own_sem,
     round_sem,
+    lm_ref,
+    rm_ref,
+    om_ref,
 ):
     row = lax.axis_index("row")
     col = lax.axis_index("col")
@@ -49,8 +52,12 @@
 
     load_a = pltpu.make_async_copy(left_ref, a_stage, load_sem.at[0])
     load_b = pltpu.make_async_copy(right_ref, b_stage, load_sem.at[1])
-    load_a.start()
-    load_b.start()
+    load_masks = [
+        pltpu.make_async_copy(src, dst, load_sem.at[2 + i])
+        for i, (src, dst) in enumerate(((lm_hbm, lm_ref), (rm_hbm, rm_ref), (om_hbm, om_ref)))
+    ]
+    for load in (*load_masks, load_a, load_b):
+        load.start()
 
     barrier = pltpu.get_barrier_semaphore()
     me = row * 16 + col
@@ -73,6 +80,8 @@
     greet(barrier, (*x_side, *y_side, *z_side, mate))
 
     x_off = pl.multiple_of(x * 512, 512)
+    for load in load_masks:
+        load.wait()
     load_a.wait()
     for j in range(4):
         for i in range(8):
@@ -389,13 +398,13 @@
 
 
 def local(left_amps, right_ints, left_mask, right_mask, result_mask):
-    smem = pl.BlockSpec(memory_space=pltpu.SMEM)
-    hbm = pl.BlockSpec(memory_space=pl.ANY)
+    hbm = pl.BlockSpec(memory_space=pltpu.HBM)
+    anywhere = pl.BlockSpec(memory_space=pl.ANY)
     strips = pl.pallas_call(
         contract,
         out_shape=jax.ShapeDtypeStruct((128, 8, 1024), BF16),
-        in_specs=[smem, smem, smem, hbm, hbm],
-        out_specs=hbm,
+        in_specs=[hbm] * 5,
+        out_specs=anywhere,
         scratch_shapes=[
             pltpu.VMEM((4, 1024, 2048), BF16),
             pltpu.VMEM((4, 2048, 1024), BF16),
@@ -403,7 +412,7 @@
             pltpu.VMEM((1024, 1024), BF16),
             pltpu.VMEM((1024, 1024), F32),
             pltpu.VMEM((128, 8, 1024), BF16),
-            pltpu.SemaphoreType.DMA((2,)),
+            pltpu.SemaphoreType.DMA((5,)),
             pltpu.SemaphoreType.DMA((40,)),
             pltpu.SemaphoreType.DMA((40,)),
             pltpu.SemaphoreType.DMA((25,)),
@@ -412,18 +421,27 @@
             pltpu.SemaphoreType.DMA(()),
             pltpu.SemaphoreType.DMA(()),
             pltpu.SemaphoreType.REGULAR((6,)),
+            pltpu.SMEM((4, 8), jnp.int32),
+            pltpu.SMEM((8, 8), jnp.int32),
+            pltpu.SMEM((8, 8), jnp.int32),
         ],
         compiler_params=pltpu.CompilerParams(
-            collective_id=0, has_side_effects=True, vmem_limit_bytes=60 * MIB
+            collective_id=0, has_side_effects=True, vmem_limit_bytes=46 * MIB
         ),
         name="contract",
-    )(left_mask.T, right_mask, result_mask, left_amps, right_ints)
+    )(
+        *(
+            pltpu.with_memory_space_constraint(array, pltpu.HBM)
+            for array in (left_mask.T, right_mask, result_mask, left_amps, right_ints)
+        )
+    )
     return pl.pallas_call(
         flatten_kernel,
         grid=(2,),
         in_specs=[pl.BlockSpec((64, 8, 1024), lambda p: (p, 0, 0))],
         out_specs=pl.BlockSpec((64, 8192), lambda p: (p, 0)),
         out_shape=jax.ShapeDtypeStruct((128, 8192), BF16),
+        compiler_params=pltpu.CompilerParams(vmem_limit_bytes=12 * MIB),
         name="flatten",
     )(strips)
 

time: 126 us -> 124 us (0.984)
  Pallas kernels: 126 us -> 124 us
where the time goes in v5:
time: 124 us
  Pallas kernels  124 us (100%)
    pallas_call x1, Pallas kernels, local(): pl.pallas_call(contract, out_shape=jax.ShapeDtypeStruct((128, 8, 1024), B...  122 us

profile of v5, /device:TPU:1, one launch (start us, length us, event | category | flops | bytes accessed | tf_op | source)
XLA Modules:
  0.0 124.0 jit_solution(16804572731079344677)
XLA Ops:
  0.0 122.4 %contract.1.in_ref = bf16[128,8,1024]{2,1,0:T(8,128)(2,1)S(1)} custom-call(s32[4,8]{1,0:T(4,128)} %bitcast.1, s32[8,8]{1,0:T(8,128)} %rm_hbm.1, s32[8,8]{1,0:T(8,128)} %om_hbm.1, bf16[1024,512]{1,0:T(8,128)(2,1)} %left_ref.1, bf16[1024,1024]{1,0:T(8,128)(2,1)} %right_ref.1), custom_call_target="tpu_custom_call" | custom-call | tf_op jit(solution)/shard_map/contract/pallas_call | solution.py:403
  122.4 1.6 %flatten.1 = bf16[128,8192]{1,0:T(8,128)(2,1)} custom-call(bf16[128,8,1024]{2,1,0:T(8,128)(2,1)S(1)} %contract.1.in_ref), custom_call_target="tpu_custom_call" | custom-call | tf_op jit(solution)/shard_map/flatten/pallas_call | solution.py:438

commit v6 on v5

--- a/solution.py
+++ b/solution.py
@@ -89,14 +89,7 @@
             rows = slice(i * TILE, (i + 1) * TILE)
             block = a_stage[rows, j * TILE : (j + 1) * TILE].astype(F32) * keep
             a_buf[y, rows, pl.ds(pl.multiple_of(x_off + j * TILE, TILE), TILE)] = block.astype(BF16)
-    load_b.wait()
-    for i in range(8):
-        rows = pl.ds(pl.multiple_of(core * 1024 + i * TILE, TILE), TILE)
-        for j in range(8):
-            keep = rm_ref[i, j].astype(F32)
-            cols = slice(j * TILE, (j + 1) * TILE)
-            block = b_stage[i * TILE : (i + 1) * TILE, cols].astype(F32) * keep
-            b_buf[z, rows, cols] = block.astype(BF16)
+    total[0:256, :] = jnp.zeros((256, 1024), F32)
 
     pl.semaphore_wait(barrier, 7)
 
@@ -233,15 +226,23 @@
     for step in steps:
         for half in halves:
             a_go(half, 0, 0, 0, step, None)
+    for step in steps:
+        for half in halves:
+            a_go(half, 0, 0, 1, step, None)
+    load_b.wait()
+    for i in range(8):
+        rows = pl.ds(pl.multiple_of(core * 1024 + i * TILE, TILE), TILE)
+        for j in range(8):
+            keep = rm_ref[i, j].astype(F32)
+            cols = slice(j * TILE, (j + 1) * TILE)
+            block = b_stage[i * TILE : (i + 1) * TILE, cols].astype(F32) * keep
+            b_buf[z, rows, cols] = block.astype(BF16)
+    total[256:, :] = jnp.zeros((768, 1024), F32)
+    pass_on(0)
     for piece in (0, 1):
         b_go(0, piece, 1)
         b_go(0, 3 - piece, -1)
-    for step in steps:
-        for half in halves:
-            a_go(half, 0, 0, 1, step, None)
     b_go(0, 0, 0, 4)
-    pass_on(0)
-    total[...] = jnp.zeros_like(total)
 
     for half in halves:
         a_wait(half, -1, 0)

time: 124 us -> 123 us (level)
  no operation moved by 1% of the time
where the time goes in v6:
time: 123 us
  Pallas kernels  123 us (100%)
    pallas_call x1, Pallas kernels, local(): pl.pallas_call(contract, out_shape=jax.ShapeDtypeStruct((128, 8, 1024), B...  122 us

profile of v6, /device:TPU:1, one launch (start us, length us, event | category | flops | bytes accessed | tf_op | source)
XLA Modules:
  0.0 123.1 jit_solution(13994015334217192737)
XLA Ops:
  0.0 121.5 %contract.1.in_ref = bf16[128,8,1024]{2,1,0:T(8,128)(2,1)S(1)} custom-call(s32[4,8]{1,0:T(4,128)} %bitcast.1, s32[8,8]{1,0:T(8,128)} %rm_hbm.1, s32[8,8]{1,0:T(8,128)} %om_hbm.1, bf16[1024,512]{1,0:T(8,128)(2,1)} %left_ref.1, bf16[1024,1024]{1,0:T(8,128)(2,1)} %right_ref.1), custom_call_target="tpu_custom_call" | custom-call | tf_op jit(solution)/shard_map/contract/pallas_call | solution.py:404
  121.5 1.6 %flatten.1 = bf16[128,8192]{1,0:T(8,128)(2,1)} custom-call(bf16[128,8,1024]{2,1,0:T(8,128)(2,1)S(1)} %contract.1.in_ref), custom_call_target="tpu_custom_call" | custom-call | tf_op jit(solution)/shard_map/flatten/pallas_call | solution.py:439

commit v7 on v6

--- a/solution.py
+++ b/solution.py
@@ -342,19 +342,20 @@
                 found.append((wrap(z + dz) * 2 + there_core, there_y))
         return found
 
-    def finish(part):
+    def finish(part, side):
+        cols = slice(side * 512, side * 512 + 512)
         strips = strips_of(part)
         rows = [pl.ds(pl.multiple_of(g * TILE + v * 32, 32), 32) for g, v in strips]
         group, k = wrap(y + 2), depth(2)
 
-        value = jnp.concatenate([total[r, :] for r in rows], axis=0)
+        value = jnp.concatenate([total[r, cols] for r in rows], axis=0)
         lhs = jnp.concatenate([a_buf[group, r, k] for r in rows], axis=0)
-        value += jnp.dot(lhs, b_buf[group, k, :], preferred_element_type=F32)
+        value += jnp.dot(lhs, b_buf[group, k, cols], preferred_element_type=F32)
         for i, (g, v) in enumerate(strips):
-            for j in range(8):
-                keep = om_ref[g, j].astype(F32)
+            for j in range(4):
+                keep = om_ref[g, side * 4 + j].astype(F32)
                 block = value[i * 32 : (i + 1) * 32, j * TILE : (j + 1) * TILE] * keep
-                kept[pl.ds(g * 16 + v * 4, 4), :, j * TILE : (j + 1) * TILE] = block.reshape(
+                kept[pl.ds(g * 16 + v * 4, 4), :, pl.ds((side * 4 + j) * TILE, TILE)] = block.reshape(
                     4, 8, TILE
                 ).astype(BF16)
 
@@ -376,10 +377,12 @@
 
         lax.fori_loop(1 if part == 0 else 0, 32, one, 0)
 
-    finish(order[0])
+    finish(order[0], 0)
+    finish(order[0], 1)
     for now, later in zip(order, order[1:]):
-        finish(later)
+        finish(later, 0)
         hand_out(now)
+        finish(later, 1)
     hand_out(order[-1])
     own = pltpu.make_async_copy(kept.at[me], out_ref.at[me], own_sem)
     own.start()

time: 123 us -> 123 us (level)
  no operation moved by 1% of the time
where the time goes in v7:
time: 123 us
  Pallas kernels  123 us (100%)
    pallas_call x1, Pallas kernels, local(): pl.pallas_call(contract, out_shape=jax.ShapeDtypeStruct((128, 8, 1024), B...  121 us

profile of v7, /device:TPU:1, one launch (start us, length us, event | category | flops | bytes accessed | tf_op | source)
XLA Modules:
  0.0 122.9 jit_solution(11423294382798244275)
XLA Ops:
  0.0 121.3 %contract.1.in_ref = bf16[128,8,1024]{2,1,0:T(8,128)(2,1)S(1)} custom-call(s32[4,8]{1,0:T(4,128)} %bitcast.1, s32[8,8]{1,0:T(8,128)} %rm_hbm.1, s32[8,8]{1,0:T(8,128)} %om_hbm.1, bf16[1024,512]{1,0:T(8,128)(2,1)} %left_ref.1, bf16[1024,1024]{1,0:T(8,128)(2,1)} %right_ref.1), custom_call_target="tpu_custom_call" | custom-call | tf_op jit(solution)/shard_map/contract/pallas_call | solution.py:407
  121.4 1.6 %flatten.1 = bf16[128,8192]{1,0:T(8,128)(2,1)} custom-call(bf16[128,8,1024]{2,1,0:T(8,128)(2,1)S(1)} %contract.1.in_ref), custom_call_target="tpu_custom_call" | custom-call | tf_op jit(solution)/shard_map/flatten/pallas_call | solution.py:442
